TPU v7x, 32 devices: a whole 2x2x4 slice. The times are simulated.
32 devices in a mesh: aa: 4 (over z), ba: 8 (over y, x, core).
Axes of the slice: x: 2, y: 2, z: 4, core: 2. Of those that a mesh axis runs over, the one named last changes fastest.
Arguments:
- feats: bfloat16 [4, 32, 128, 256], P('aa', 'ba'), may hold values from -6 to 6
- conv_one: bfloat16 [3, 3, 3, 256, 256], replicated, may hold values from -0.078125 to 0.078125
- bias_one: float32 [256], replicated, may hold values from -3 to 3
- conv_two: bfloat16 [3, 3, 3, 256, 256], replicated, may hold values from -0.078125 to 0.078125
- bias_two: float32 [256], replicated, may hold values from -3 to 3
- patch_weight: bfloat16 [2, 2, 256, 128], replicated, may hold values from -0.1875 to 0.1875
- patch_bias: float32 [128], replicated, may hold values from -3 to 3
- embed_weight: bfloat16 [128, 2048], replicated, may hold values from -0.5 to 0.5
- embed_bias: float32 [2048], replicated, may hold values from -6 to 6
- norm_gain: float32 [2048], replicated, may hold values from 0.1 to 1.9
- w_query: bfloat16 [2048, 2048], P(None, 'ba'), may hold values from -2 to 2
- w_key: bfloat16 [2048, 2048], P(None, 'ba'), may hold values from -2 to 2
- w_value: bfloat16 [2048, 2048], P(None, 'ba'), may hold values from -0.125 to 0.125
- w_velocity: bfloat16 [2048, 128], P('ba'), may hold values from -0.5 to 0.5
Outputs:
- velocity: float32 [4096, 128], P(('aa', 'ba'))
All inputs are finite; a program needn't handle non-finite values.
Results may differ from a plain program's by a relative error of at most 0.035.
Values may be sent and summed in bfloat16 or wider, within the bound.
A program may use at most 128 MiB of HBM per device.

v0:
```python
import math
import jax
import jax.numpy as jnp
from jax import lax
from jax.sharding import PartitionSpec as P

HEAD_DIM = 64


def with_halo(cells, sides, width):
    for axis, dim in sides:
        count = lax.axis_size(axis)
        ends = count - 1
        head = lax.slice_in_dim(cells, 0, width, axis=dim)
        tail = lax.slice_in_dim(cells, cells.shape[dim] - width, cells.shape[dim], axis=dim)
        cells = jnp.concatenate(
            [
                lax.ppermute(tail, axis, [(i, (i + 1) % count) for i in range(ends)]),
                cells,
                lax.ppermute(head, axis, [((i + 1) % count, i) for i in range(ends)]),
            ],
            axis=dim,
        )
    return cells


def convolve(field, kernel, bias):
    frames, rows, width, chans = field.shape
    padded = with_halo(field, (("aa", 0), ("ba", 1)), 1)
    padded = jnp.pad(padded, ((0, 0), (0, 0), (1, 1), (0, 0)))
    total = jnp.zeros((frames * rows * width, kernel.shape[-1]), jnp.float32)
    for shift_t in range(3):
        for shift_r in range(3):
            window = padded[shift_t : shift_t + frames, shift_r : shift_r + rows]
            stacked = jnp.concatenate(
                [window[:, :, shift_w : shift_w + width] for shift_w in range(3)], axis=-1
            )
            total = total + jnp.dot(
                stacked.reshape(-1, 3 * chans),
                kernel[shift_t, shift_r].reshape(3 * chans, -1),
                preferred_element_type=jnp.float32,
            )
    return (total + bias).reshape(frames, rows, width, -1)


def patchify(field, weight, bias):
    frames, rows, width, chans = field.shape
    blocks = (
        field.reshape(frames, rows // 2, 2, width // 2, 2, chans)
        .transpose(0, 1, 3, 2, 4, 5)
        .reshape(-1, 4 * chans)
    )
    return (
        jnp.dot(blocks, weight.reshape(4 * chans, -1), preferred_element_type=jnp.float32) + bias
    ).astype(jnp.bfloat16)


def normalize(latent_rows, embed_weight, embed_bias, norm_gain):
    hidden = jnp.dot(latent_rows, embed_weight, preferred_element_type=jnp.float32) + embed_bias
    center = hidden - hidden.mean(-1, keepdims=True)
    spread = (center * center).mean(-1, keepdims=True)
    return (center * lax.rsqrt(spread + 1e-05) * norm_gain).astype(jnp.bfloat16)


def attend(queries, keys, values):
    rows, width = queries.shape
    heads = width // HEAD_DIM
    scale = HEAD_DIM ** (-0.5)
    query_heads = queries.reshape(rows, heads, HEAD_DIM)
    start_state = (
        jnp.full((heads, rows), -jnp.inf, jnp.float32),
        jnp.zeros((heads, rows), jnp.float32),
        jnp.zeros((rows, heads, HEAD_DIM), jnp.float32),
    )
    key_rows = lax.all_gather(keys, "aa", axis=0, tiled=True)
    value_rows = lax.all_gather(values, "aa", axis=0, tiled=True)
    count = key_rows.shape[0]
    block = math.gcd(count, 1024)

    def one_step(index, state):
        best, denom, accum = state
        key_block = lax.dynamic_slice_in_dim(key_rows, index * block, block, 0).reshape(
            block, heads, HEAD_DIM
        )
        value_block = lax.dynamic_slice_in_dim(value_rows, index * block, block, 0).reshape(
            block, heads, HEAD_DIM
        )
        scores = (
            jnp.einsum("qhd,khd->hqk", query_heads, key_block, preferred_element_type=jnp.float32)
            * scale
        )
        peak = jnp.maximum(best, scores.max(-1))
        probs = jnp.exp(scores - peak[..., None])
        fade = jnp.exp(best - peak)
        denom = denom * fade + probs.sum(-1)
        accum = accum * fade.T[..., None] + jnp.einsum(
            "hqk,khd->qhd",
            probs.astype(jnp.bfloat16),
            value_block,
            preferred_element_type=jnp.float32,
        )
        return (peak, denom, accum)

    best, denom, accum = lax.fori_loop(0, count // block, one_step, start_state)
    return (accum / denom.T[..., None]).reshape(rows, width).astype(jnp.bfloat16)


def on_device(
    feats,
    conv_one,
    bias_one,
    conv_two,
    bias_two,
    patch_weight,
    patch_bias,
    embed_weight,
    embed_bias,
    norm_gain,
    w_query,
    w_key,
    w_value,
    w_velocity,
):
    first = jax.nn.gelu(convolve(feats, conv_one, bias_one), approximate=False).astype(jnp.bfloat16)
    second = (
        first.astype(jnp.float32)
        + jax.nn.gelu(convolve(first, conv_two, bias_two), approximate=False)
    ).astype(jnp.bfloat16)
    latents = patchify(second, patch_weight, patch_bias)
    width = w_query.shape[1]
    w_joined = jnp.concatenate([w_query, w_key, w_value], axis=1)
    joined = jnp.dot(
        normalize(
            lax.all_gather(latents, "ba", axis=0, tiled=True), embed_weight, embed_bias, norm_gain
        ),
        w_joined,
        preferred_element_type=jnp.float32,
    ).astype(jnp.bfloat16)
    attended = attend(joined[:, :width], joined[:, width : 2 * width], joined[:, 2 * width :])
    return lax.psum_scatter(
        jnp.dot(attended, w_velocity, preferred_element_type=jnp.float32).astype(jnp.bfloat16),
        "ba",
        scatter_dimension=0,
        tiled=True,
    ).astype(jnp.float32)


def solution(mesh):
    return jax.shard_map(
        on_device,
        mesh=mesh,
        in_specs=(
            P("aa", "ba", None, None),
            P(),
            P(),
            P(),
            P(),
            P(),
            P(),
            P(),
            P(),
            P(),
            P(None, "ba"),
            P(None, "ba"),
            P(None, "ba"),
            P("ba", None),
        ),
        out_specs=P(("aa", "ba"), None),
        check_vma=False,
    )
```

profile of v0, /device:TPU:0, one launch (start us, length us, event | category | flops | bytes accessed | tf_op | source)
XLA Modules:
  0.0 332.6 jit_solution(549942878547130094)
XLA Ops:
  6.5 5.1 %collective-permute-start = (bf16[1,4,128,256]{3,2,1,0:T(8,128)(2,1)}, bf16[1,4,128,256]{3,2,1,0:T(8,128)(2,1)S(1)}, u32[]{:S(2)}, u32[]{:S(2)}) collective-permute-start(bf16[1,4,128,256]{3,2,1,0:T(8,128)(2,1)} %param.16), channel_id=1, source_target_pairs={{0,8},{8,16},{16,24},{1,9},{9,17},{17,25},{2,10},{10,18},{18,26},{... | collective-permute-start | bytes 786440 | tf_op jit(solution)/shard_map/ppermute | solution.py:18
  12.9 4.5 %collective-permute-done = bf16[1,4,128,256]{3,2,1,0:T(8,128)(2,1)S(1)} collective-permute-done((bf16[1,4,128,256]{3,2,1,0:T(8,128)(2,1)}, bf16[1,4,128,256]{3,2,1,0:T(8,128)(2,1)S(1)}, u32[]{:S(2)}, u32[]{:S(2)}) %collective-permute-start) | collective-permute-done | bytes 262176 | tf_op jit(solution)/shard_map/ppermute | solution.py:18
  18.5 3.0 collective-permute-done.1
  24.2 2.2 fusion.102
  26.4 1.6 collective-permute-done.3
  33.6 2.1 fusion.69
  36.8 3.5 %collective-permute-start.4 = (bf16[1,4,128,256]{3,2,1,0:T(8,128)(2,1)S(1)}, bf16[1,4,128,256]{3,2,1,0:T(8,128)(2,1)S(1)}, u32[]{:S(2)}, u32[]{:S(2)}) collective-permute-start(bf16[1,4,128,256]{3,2,1,0:T(8,128)(2,1)S(1)} %fusion.66), channel_id=1, source_target_pairs={{0,8},{8,16},{16,24},{1,9},{9,17},{17,25},{2,10},{10,18},{18,26},{... | collective-permute-start | bytes 786440 | tf_op jit(solution)/shard_map/ppermute | solution.py:18
  41.6 2.6 collective-permute-done.4
  44.1 4.4 %collective-permute-done.5 = bf16[1,4,128,256]{3,2,1,0:T(8,128)(2,1)S(1)} collective-permute-done((bf16[1,4,128,256]{3,2,1,0:T(8,128)(2,1)S(1)}, bf16[1,4,128,256]{3,2,1,0:T(8,128)(2,1)S(1)}, u32[]{:S(2)}, u32[]{:S(2)}) %collective-permute-start.5) | collective-permute-done | bytes 262176 | tf_op jit(solution)/shard_map/ppermute | solution.py:20
  49.3 5.3 %collective-permute-start.6 = (bf16[3,1,128,256]{3,2,1,0:T(8,128)(2,1)}, bf16[3,1,128,256]{3,2,1,0:T(8,128)(2,1)}, u32[]{:S(2)}, u32[]{:S(2)}) collective-permute-start(bf16[3,1,128,256]{3,2,1,0:T(8,128)(2,1)} %get-tuple-element.246), channel_id=1, source_target_pairs={{0,1},{1,2},{2,3},{3,4},{4,5},{5,6},{6,7},{8,9},{9,10},{10,11},{11... | collective-permute-start | bytes 589832 | tf_op jit(solution)/shard_map/ppermute | solution.py:18
  54.6 1.5 collective-permute-start.7
  56.1 1.7 fusion.101
  59.6 1.5 select_maximum_fusion.1
  70.8 2.2 fusion.98
  74.7 15.0 %all_gather.9 = bf16[1024,128]{1,0:T(8,128)(2,1)S(1)} all-gather(bf16[128,128]{1,0:T(8,128)(2,1)S(1)} %fusion.31), channel_id=1, replica_groups=mesh['aa'=4,'ba'=8] {'ba'}, dimensions={0}, use_global_device_ids=true | all-gather | bytes 294912 | tf_op jit(solution)/shard_map/all_gather | solution.py:134
  92.9 4.3 %fusion.25 = bf16[1024,768]{0,1:T(8,128)(2,1)S(1)} fusion(bf16[2048,256]{1,0:T(8,128)(2,1)S(1)} %copy-done.16, bf16[2048,256]{1,0:T(8,128)(2,1)S(1)} %copy-done.17, bf16[2048,256]{1,0:T(8,128)(2,1)S(1)} %copy-done.18, f32[1024,2048]{1,0:T(8,128)S(1)} %get-tuple-element.255, f32[2048]{0:T(1024)S(1)} %copy-done.19, f32[1024]{0:T(1024)S(1)} %add_rsqrt_fusion, ...), kind=kOutput, calls=%fused_computation.33 | convolution fusion | flops 3241934848 | bytes 13131776 | tf_op jit(solution)/shard_map/dot_general | solution.py:132
  99.4 43.0 %all-gather.3.cloned.1.call-done = bf16[4096,256]{0,1:T(8,128)(2,1)} async-done(((bf16[1024,256]{0,1:T(8,128)(2,1)}), bf16[4096,256]{0,1:T(8,128)(2,1)}) %all-gather.3.cloned.1.call-update) | async-done | bytes 2097168 | tf_op jit(solution)/shard_map/all_gather | solution.py:75
  142.4 46.1 %all-gather.5.cloned.1.call-done = bf16[4096,256]{0,1:T(8,128)(2,1)} async-done(((bf16[1024,256]{0,1:T(8,128)(2,1)}), bf16[4096,256]{0,1:T(8,128)(2,1)}) %all-gather.5.cloned.1.call-update) | async-done | bytes 2097168 | tf_op jit(solution)/shard_map/all_gather | solution.py:76
  188.4 101.7 %while.18 = (s32[]{:T(128)}, f32[4,1024]{1,0:T(4,128)S(1)}, f32[4,1024]{1,0:T(4,128)S(1)}, f32[1024,4,64]{0,2,1:T(8,128)S(1)}, bf16[4096,256]{0,1:T(8,128)(2,1)}...) while((s32[]{:T(128)}, f32[4,1024]{1,0:T(4,128)S(1)}, ...), condition=%wide.region_5.6_spmd.clone, body=%wide.region_2.5_spmd.clone.sunk | while | flops 1108107264 | bytes 56361128 | solution.py:104
  189.7 8.1 %bitcast_reduce_fusion.2 = (f32[4,1024]{1,0:T(4,128)S(1)}, f32[4,1024,1024]{2,1,0:T(8,128)}) fusion(bf16[1024,4,64]{0,2,1:T(8,128)(2,1)S(1)} %bitcast.131, bf16[1024,4,64]{0,2,1:T(8,128)(2,1)S(1)} %get-tuple-element.340), kind=kOutput, calls=%fused_computation.1.clone.1 | convolution fusion | flops 545255424 | bytes 17842176 | tf_op jit(solution)/shard_map/while/body/eval_jaxpr/qhd,khd->hqk/dot_general | solution.py:89
  197.9 7.4 %fusion.168 = f32[1024,4,64]{0,2,1:T(8,128)S(1)} fusion(bf16[1024,4,64]{0,2,1:T(8,128)(2,1)S(1)} %bitcast.132, f32[4,1024,1024]{2,1,0:T(8,128)} %get-tuple-element.310, f32[4,1024]{1,0:T(4,128)S(1)} %get-tuple-element.336, f32[1024,4,64]{0,2,1:T(8,128)S(1)} %get-tuple-element.327, f32[1024,4]{0,1:T(4,128)S(1)} %get-tuple-element.312, pred[]{:T(512)S(6)} %compare.43), kind=kOutput, calls=%fused_computation.7.clone.1 | convolution fusion | flops 550240256 | bytes 19431424 | tf_op jit(solution)/shard_map/while/body/eval_jaxpr/hqk,khd->qhd/dot_general | solution.py:96
  205.2 8.5 %fusion.166 = f32[4,1024]{1,0:T(4,128)S(1)} fusion(f32[4,1024,1024]{2,1,0:T(8,128)} %get-tuple-element.310, f32[4,1024]{1,0:T(4,128)S(1)} %get-tuple-element.336), kind=kLoop, calls=%fused_computation.4.clone.1 | loop fusion | flops 12578816 | bytes 16809984 | tf_op jit(solution)/shard_map/while/body/eval_jaxpr/reduce_sum | solution.py:95
  215.1 8.1 %bitcast_reduce_fusion.2 = (f32[4,1024]{1,0:T(4,128)S(1)}, f32[4,1024,1024]{2,1,0:T(8,128)}) fusion(bf16[1024,4,64]{0,2,1:T(8,128)(2,1)S(1)} %bitcast.131, bf16[1024,4,64]{0,2,1:T(8,128)(2,1)S(1)} %get-tuple-element.340), kind=kOutput, calls=%fused_computation.1.clone.1 | convolution fusion | flops 545255424 | bytes 17842176 | tf_op jit(solution)/shard_map/while/body/eval_jaxpr/qhd,khd->hqk/dot_general | solution.py:89
  223.3 7.4 %fusion.168 = f32[1024,4,64]{0,2,1:T(8,128)S(1)} fusion(bf16[1024,4,64]{0,2,1:T(8,128)(2,1)S(1)} %bitcast.132, f32[4,1024,1024]{2,1,0:T(8,128)} %get-tuple-element.310, f32[4,1024]{1,0:T(4,128)S(1)} %get-tuple-element.336, f32[1024,4,64]{0,2,1:T(8,128)S(1)} %get-tuple-element.327, f32[1024,4]{0,1:T(4,128)S(1)} %get-tuple-element.312, pred[]{:T(512)S(6)} %compare.43), kind=kOutput, calls=%fused_computation.7.clone.1 | convolution fusion | flops 550240256 | bytes 19431424 | tf_op jit(solution)/shard_map/while/body/eval_jaxpr/hqk,khd->qhd/dot_general | solution.py:96
  230.7 8.5 %fusion.166 = f32[4,1024]{1,0:T(4,128)S(1)} fusion(f32[4,1024,1024]{2,1,0:T(8,128)} %get-tuple-element.310, f32[4,1024]{1,0:T(4,128)S(1)} %get-tuple-element.336), kind=kLoop, calls=%fused_computation.4.clone.1 | loop fusion | flops 12578816 | bytes 16809984 | tf_op jit(solution)/shard_map/while/body/eval_jaxpr/reduce_sum | solution.py:95
  240.5 8.1 %bitcast_reduce_fusion.2 = (f32[4,1024]{1,0:T(4,128)S(1)}, f32[4,1024,1024]{2,1,0:T(8,128)}) fusion(bf16[1024,4,64]{0,2,1:T(8,128)(2,1)S(1)} %bitcast.131, bf16[1024,4,64]{0,2,1:T(8,128)(2,1)S(1)} %get-tuple-element.340), kind=kOutput, calls=%fused_computation.1.clone.1 | convolution fusion | flops 545255424 | bytes 17842176 | tf_op jit(solution)/shard_map/while/body/eval_jaxpr/qhd,khd->hqk/dot_general | solution.py:89
  248.7 7.4 %fusion.168 = f32[1024,4,64]{0,2,1:T(8,128)S(1)} fusion(bf16[1024,4,64]{0,2,1:T(8,128)(2,1)S(1)} %bitcast.132, f32[4,1024,1024]{2,1,0:T(8,128)} %get-tuple-element.310, f32[4,1024]{1,0:T(4,128)S(1)} %get-tuple-element.336, f32[1024,4,64]{0,2,1:T(8,128)S(1)} %get-tuple-element.327, f32[1024,4]{0,1:T(4,128)S(1)} %get-tuple-element.312, pred[]{:T(512)S(6)} %compare.43), kind=kOutput, calls=%fused_computation.7.clone.1 | convolution fusion | flops 550240256 | bytes 19431424 | tf_op jit(solution)/shard_map/while/body/eval_jaxpr/hqk,khd->qhd/dot_general | solution.py:96
  256.1 8.5 %fusion.166 = f32[4,1024]{1,0:T(4,128)S(1)} fusion(f32[4,1024,1024]{2,1,0:T(8,128)} %get-tuple-element.310, f32[4,1024]{1,0:T(4,128)S(1)} %get-tuple-element.336), kind=kLoop, calls=%fused_computation.4.clone.1 | loop fusion | flops 12578816 | bytes 16809984 | tf_op jit(solution)/shard_map/while/body/eval_jaxpr/reduce_sum | solution.py:95
  266.0 8.1 %bitcast_reduce_fusion.2 = (f32[4,1024]{1,0:T(4,128)S(1)}, f32[4,1024,1024]{2,1,0:T(8,128)}) fusion(bf16[1024,4,64]{0,2,1:T(8,128)(2,1)S(1)} %bitcast.131, bf16[1024,4,64]{0,2,1:T(8,128)(2,1)S(1)} %get-tuple-element.340), kind=kOutput, calls=%fused_computation.1.clone.1 | convolution fusion | flops 545255424 | bytes 17842176 | tf_op jit(solution)/shard_map/while/body/eval_jaxpr/qhd,khd->hqk/dot_general | solution.py:89
  274.1 7.4 %fusion.168 = f32[1024,4,64]{0,2,1:T(8,128)S(1)} fusion(bf16[1024,4,64]{0,2,1:T(8,128)(2,1)S(1)} %bitcast.132, f32[4,1024,1024]{2,1,0:T(8,128)} %get-tuple-element.310, f32[4,1024]{1,0:T(4,128)S(1)} %get-tuple-element.336, f32[1024,4,64]{0,2,1:T(8,128)S(1)} %get-tuple-element.327, f32[1024,4]{0,1:T(4,128)S(1)} %get-tuple-element.312, pred[]{:T(512)S(6)} %compare.43), kind=kOutput, calls=%fused_computation.7.clone.1 | convolution fusion | flops 550240256 | bytes 19431424 | tf_op jit(solution)/shard_map/while/body/eval_jaxpr/hqk,khd->qhd/dot_general | solution.py:96
  281.5 8.5 %fusion.166 = f32[4,1024]{1,0:T(4,128)S(1)} fusion(f32[4,1024,1024]{2,1,0:T(8,128)} %get-tuple-element.310, f32[4,1024]{1,0:T(4,128)S(1)} %get-tuple-element.336), kind=kLoop, calls=%fused_computation.4.clone.1 | loop fusion | flops 12578816 | bytes 16809984 | tf_op jit(solution)/shard_map/while/body/eval_jaxpr/reduce_sum | solution.py:95
  292.0 32.6 %reduce-scatter.2.cloned.1.call-done = bf16[128,128]{1,0:T(8,128)(2,1)} async-done(((bf16[1024,128]{1,0:T(8,128)(2,1)}), bf16[128,128]{1,0:T(8,128)(2,1)}) %reduce-scatter.2.cloned.1.call-update) | async-done | bytes 32784 | tf_op jit(solution)/shard_map/reduce_scatter | solution.py:140
  (124 shorter events, 40.4 us)
Async XLA Ops:
  6.5 83.1 %copy-start = (bf16[128,2048]{1,0:T(8,128)(2,1)S(1)}, bf16[128,2048]{1,0:T(8,128)(2,1)}, u32[]{:S(2)}) copy-start(bf16[128,2048]{1,0:T(8,128)(2,1)} %param.23) | copy-start | bytes 1572868
  6.5 135.8 %all-gather.3.cloned.1.call-start = ((), (), s32[]{:S(2)}) async-start(), calls=%async_computation.1 | async-start | bytes 2621440 | tf_op jit(solution)/shard_map/all_gather | solution.py:75
  6.5 10.9 %collective-permute-start = (bf16[1,4,128,256]{3,2,1,0:T(8,128)(2,1)}, bf16[1,4,128,256]{3,2,1,0:T(8,128)(2,1)S(1)}, u32[]{:S(2)}, u32[]{:S(2)}) collective-permute-start(bf16[1,4,128,256]{3,2,1,0:T(8,128)(2,1)} %param.16), channel_id=1, source_target_pairs={{0,8},{8,16},{16,24},{1,9},{9,17},{17,25},{2,10},{10,18},{18,26},{... | collective-permute-start | bytes 786440 | tf_op jit(solution)/shard_map/ppermute | solution.py:18
  11.6 9.9 %collective-permute-start.1 = (bf16[1,4,128,256]{3,2,1,0:T(8,128)(2,1)}, bf16[1,4,128,256]{3,2,1,0:T(8,128)(2,1)S(1)}, u32[]{:S(2)}, u32[]{:S(2)}) collective-permute-start(bf16[1,4,128,256]{3,2,1,0:T(8,128)(2,1)} %param.16), channel_id=1, source_target_pairs={{8,0},{16,8},{24,16},{9,1},{17,9},{25,17},{10,2},{18,10},{26,18},{... | collective-permute-start | bytes 786440 | tf_op jit(solution)/shard_map/ppermute | solution.py:20
  21.6 4.8 %collective-permute-start.2 = (bf16[3,1,128,256]{3,2,1,0:T(8,128)(2,1)S(1)}, bf16[3,1,128,256]{3,2,1,0:T(8,128)(2,1)S(1)}, u32[]{:S(2)}, u32[]{:S(2)}) collective-permute-start(bf16[3,1,128,256]{3,2,1,0:T(8,128)(2,1)S(1)} %get-tuple-element.248), channel_id=1, source_target_pairs={{0,1},{1,2},{2,3},{3,4},{4,5},{5,6},{6,7},{8,9},{9,10},{10,11},{11... | collective-permute-start | bytes 589832 | tf_op jit(solution)/shard_map/ppermute | solution.py:18
  22.9 5.1 %collective-permute-start.3 = (bf16[3,1,128,256]{3,2,1,0:T(8,128)(2,1)S(1)}, bf16[3,1,128,256]{3,2,1,0:T(8,128)(2,1)S(1)}, u32[]{:S(2)}, u32[]{:S(2)}) collective-permute-start(bf16[3,1,128,256]{3,2,1,0:T(8,128)(2,1)S(1)} %get-tuple-element.247), channel_id=1, source_target_pairs={{1,0},{2,1},{3,2},{4,3},{5,4},{6,5},{7,6},{9,8},{10,9},{11,10},{12... | collective-permute-start | bytes 589832 | tf_op jit(solution)/shard_map/ppermute | solution.py:20
  28.5 1.0 copy-start.10
  33.6 22.5 %copy-start.2 = (bf16[3,3,3,256,256]{4,3,2,1,0:T(8,128)(2,1)S(1)}, bf16[3,3,3,256,256]{4,3,2,1,0:T(8,128)(2,1)}, u32[]{:S(2)}) copy-start(bf16[3,3,3,256,256]{4,3,2,1,0:T(8,128)(2,1)} %param.19) | copy-start | bytes 10616836
  36.8 7.3 %collective-permute-start.4 = (bf16[1,4,128,256]{3,2,1,0:T(8,128)(2,1)S(1)}, bf16[1,4,128,256]{3,2,1,0:T(8,128)(2,1)S(1)}, u32[]{:S(2)}, u32[]{:S(2)}) collective-permute-start(bf16[1,4,128,256]{3,2,1,0:T(8,128)(2,1)S(1)} %fusion.66), channel_id=1, source_target_pairs={{0,8},{8,16},{16,24},{1,9},{9,17},{17,25},{2,10},{10,18},{18,26},{... | collective-permute-start | bytes 786440 | tf_op jit(solution)/shard_map/ppermute | solution.py:18
  40.3 8.3 %collective-permute-start.5 = (bf16[1,4,128,256]{3,2,1,0:T(8,128)(2,1)S(1)}, bf16[1,4,128,256]{3,2,1,0:T(8,128)(2,1)S(1)}, u32[]{:S(2)}, u32[]{:S(2)}) collective-permute-start(bf16[1,4,128,256]{3,2,1,0:T(8,128)(2,1)S(1)} %fusion.66), channel_id=1, source_target_pairs={{8,0},{16,8},{24,16},{9,1},{17,9},{25,17},{10,2},{18,10},{26,18},{... | collective-permute-start | bytes 786440 | tf_op jit(solution)/shard_map/ppermute | solution.py:20
  49.3 9.1 %collective-permute-start.6 = (bf16[3,1,128,256]{3,2,1,0:T(8,128)(2,1)}, bf16[3,1,128,256]{3,2,1,0:T(8,128)(2,1)}, u32[]{:S(2)}, u32[]{:S(2)}) collective-permute-start(bf16[3,1,128,256]{3,2,1,0:T(8,128)(2,1)} %get-tuple-element.246), channel_id=1, source_target_pairs={{0,1},{1,2},{2,3},{3,4},{4,5},{5,6},{6,7},{8,9},{9,10},{10,11},{11... | collective-permute-start | bytes 589832 | tf_op jit(solution)/shard_map/ppermute | solution.py:18
  54.6 5.0 %collective-permute-start.7 = (bf16[3,1,128,256]{3,2,1,0:T(8,128)(2,1)}, bf16[3,1,128,256]{3,2,1,0:T(8,128)(2,1)S(1)}, u32[]{:S(2)}, u32[]{:S(2)}) collective-permute-start(bf16[3,1,128,256]{3,2,1,0:T(8,128)(2,1)} %get-tuple-element.245), channel_id=1, source_target_pairs={{1,0},{2,1},{3,2},{4,3},{5,4},{6,5},{7,6},{9,8},{10,9},{11,10},{12... | collective-permute-start | bytes 589832 | tf_op jit(solution)/shard_map/ppermute | solution.py:20
  62.0 1.1 copy-start.9
  63.1 1.0 copy-start.8
  64.5 1.0 copy-start.7
  64.8 1.1 copy-start.6
  65.9 1.0 copy-start.11
  65.9 1.1 copy-start.21
  66.3 1.1 copy-start.5
  67.3 1.0 copy-start.4
  68.3 1.0 copy-start.3
  68.7 1.0 copy-start.14
  70.8 2.7 copy-start.15
  70.8 18.9 %copy-start.12 = (f32[2048]{0:T(1024)S(1)}, f32[2048]{0:T(1024)}, u32[]{:S(2)}) copy-start(f32[2048]{0:T(1024)} %param.24) | copy-start | bytes 24580
  91.0 1.3 copy-start.16
  91.0 1.5 copy-start.17
  91.0 1.8 copy-start.18
  91.0 1.8 copy-start.19
  98.3 90.1 %all-gather.5.cloned.1.call-start = ((), (), s32[]{:S(2)}) async-start(), calls=%async_computation.2 | async-start | bytes 2621440 | tf_op jit(solution)/shard_map/all_gather | solution.py:76
  99.1 225.6 %reduce-scatter.2.cloned.1.call-start = ((), (), s32[]{:S(2)}) async-start(), calls=%async_computation.3 | async-start | bytes 294912 | tf_op jit(solution)/shard_map/reduce_scatter | solution.py:140
  290.1 0.8 copy-start.13
  290.1 35.9 %copy-start.1 = (bf16[128,2048]{1,0:T(8,128)(2,1)S(1)}, bf16[128,2048]{1,0:T(8,128)(2,1)}, u32[]{:S(2)}) copy-start(bf16[128,2048]{1,0:T(8,128)(2,1)} %param.23) | copy-start | bytes 1572868
  (1 other events, 0.7 us)
Sparse Core Ops, SparseCore 0:
  98.4 43.8 all-gather.2
  143.9 44.4 all-gather.4
  292.1 32.4 reduce-scatter.1
where the time goes:
time: 334 us; the launch traced here: 333 us
  waiting for transfers between devices  140 us (42%)
  matrix products  78.4 us (23%)
  other arithmetic  45.5 us (14%)
  starting transfers between devices  20.9 us (6%)
  local copies, waits for them, and re-layouts  19.1 us (6%)
  blocking collectives  15 us (4%)
  between operations  13.7 us (4%)
    all_gather x1, waiting for transfers between devices, attend(): value_rows = lax.all_gather(values, 'aa', axis=0, tiled=True)  46.1 us
    all_gather x1, waiting for transfers between devices, attend(): key_rows = lax.all_gather(keys, 'aa', axis=0, tiled=True)  43 us
    reduce_sum x4, other arithmetic, one_step(): denom = denom * fade + probs.sum(-1)  34.1 us
    reduce_scatter x1, waiting for transfers between devices, on_device(): lax.psum_scatter(jnp.dot(attended, w_velocity, preferred_element_type=jnp...  32.6 us
    dot_general x4, matrix products, one_step(): jnp.einsum('qhd,khd->hqk', query_heads, key_block, preferred_element_type...  32.6 us
    dot_general x4, matrix products, one_step(): jnp.einsum('hqk,khd->qhd', probs.astype(jnp.bfloat16), value_block, prefe...  29.5 us
    ppermute x4, starting transfers between devices, with_halo(): lax.ppermute(tail, axis, [(i, (i + 1) % count) for i in range(ends)])  15.2 us
    all_gather x1, blocking collectives, on_device(): lax.all_gather(latents, 'ba', axis=0, tiled=True)  15 us
  transfers between devices with their start and end apart: 11, of which 9 were waited for; matrix products, arithmetic and copies ran while one was open for 2% of the time, Pallas kernels for 0%

commit v1 on v0

--- a/solution.py
+++ b/solution.py
@@ -72,7 +72,22 @@
         jnp.zeros((heads, rows), jnp.float32),
         jnp.zeros((rows, heads, HEAD_DIM), jnp.float32),
     )
-    key_rows = lax.all_gather(keys, "aa", axis=0, tiled=True)
+    y_new, item_now, side_arr = (lax.axis_size("aa"), lax.axis_index("aa"), keys.shape[0])
+    inter, vec_out = (keys, 1)
+    while vec_out < y_new:
+        inter = jnp.concatenate(
+            [
+                inter,
+                lax.ppermute(
+                    inter,
+                    axis_name="aa",
+                    perm=tuple(((j, (j - vec_out) % y_new) for j in range(y_new))),
+                ),
+            ],
+            axis=0,
+        )
+        vec_out = 2 * vec_out
+    key_rows = jnp.roll(inter, item_now * side_arr, axis=0)
     value_rows = lax.all_gather(values, "aa", axis=0, tiled=True)
     count = key_rows.shape[0]
     block = math.gcd(count, 1024)

time: 334 us -> 352 us (1.054)
  waiting for transfers between devices: 140 us -> 150 us
  local copies, waits for them, and re-layouts: 19.1 us -> 26.2 us
    ppermute x0 -> x2, waiting for transfers between devices: none -> 60.5 us  [attend(): lax.ppermute(inter, axis_name='aa', perm=tuple(((j, (j - vec_out) % y_new...]
    all_gather x1 -> x0, waiting for transfers between devices: 43 us -> none  [attend(): key_rows = lax.all_gather(keys, 'aa', axis=0, tiled=True)]
    all_gather x1, waiting for transfers between devices: 46.1 us -> 39.1 us  [attend(): value_rows = lax.all_gather(values, 'aa', axis=0, tiled=True)]
    unnamed x46 -> x57, local copies, waits for them, and re-layouts: 5.63 us -> 8.55 us
  transfers between devices with their start and end apart: 11 -> 12, of which waited for: 9 -> 10; matrix products, arithmetic and copies ran while one was open for 2% -> 3% of each run, Pallas kernels for 0% -> 0%
where the time goes in v1:
time: 352 us; the launch traced here: 351 us
  waiting for transfers between devices  150 us (43%)
  matrix products  77.5 us (22%)
  other arithmetic  45.6 us (13%)
  local copies, waits for them, and re-layouts  26.2 us (7%)
  starting transfers between devices  22.5 us (6%)
  blocking collectives  15 us (4%)
  between operations  14.1 us (4%)
    ppermute x2, waiting for transfers between devices, attend(): lax.ppermute(inter, axis_name='aa', perm=tuple(((j, (j - vec_out) % y_new...  60.5 us
    all_gather x1, waiting for transfers between devices, attend(): value_rows = lax.all_gather(values, 'aa', axis=0, tiled=True)  39.1 us
    reduce_sum x4, other arithmetic, one_step(): denom = denom * fade + probs.sum(-1)  34.1 us
    reduce_scatter x1, waiting for transfers between devices, on_device(): lax.psum_scatter(jnp.dot(attended, w_velocity, preferred_element_type=jnp...  32.6 us
    dot_general x4, matrix products, one_step(): jnp.einsum('qhd,khd->hqk', query_heads, key_block, preferred_element_type...  32.6 us
    dot_general x4, matrix products, one_step(): jnp.einsum('hqk,khd->qhd', probs.astype(jnp.bfloat16), value_block, prefe...  29.5 us
    ppermute x4, starting transfers between devices, with_halo(): lax.ppermute(tail, axis, [(i, (i + 1) % count) for i in range(ends)])  15.2 us
    all_gather x1, blocking collectives, on_device(): lax.all_gather(latents, 'ba', axis=0, tiled=True)  15 us
  transfers between devices with their start and end apart: 12, of which 10 were waited for; matrix products, arithmetic and copies ran while one was open for 3% of the time, Pallas kernels for 0%

profile of v1, /device:TPU:0, one launch (start us, length us, event | category | flops | bytes accessed | tf_op | source)
XLA Modules:
  0.0 350.8 jit_solution(7876135027988444750)
XLA Ops:
  6.5 5.1 %collective-permute-start = (bf16[1,4,128,256]{3,2,1,0:T(8,128)(2,1)}, bf16[1,4,128,256]{3,2,1,0:T(8,128)(2,1)S(1)}, u32[]{:S(2)}, u32[]{:S(2)}) collective-permute-start(bf16[1,4,128,256]{3,2,1,0:T(8,128)(2,1)} %param.16), channel_id=1, source_target_pairs={{0,8},{8,16},{16,24},{1,9},{9,17},{17,25},{2,10},{10,18},{18,26},{... | collective-permute-start | bytes 786440 | tf_op jit(solution)/shard_map/ppermute | solution.py:18
  12.9 4.5 %collective-permute-done = bf16[1,4,128,256]{3,2,1,0:T(8,128)(2,1)S(1)} collective-permute-done((bf16[1,4,128,256]{3,2,1,0:T(8,128)(2,1)}, bf16[1,4,128,256]{3,2,1,0:T(8,128)(2,1)S(1)}, u32[]{:S(2)}, u32[]{:S(2)}) %collective-permute-start) | collective-permute-done | bytes 262176 | tf_op jit(solution)/shard_map/ppermute | solution.py:18
  18.5 3.0 collective-permute-done.1
  24.2 2.2 fusion.102
  33.5 2.1 fusion.69
  36.8 3.5 collective-permute-start.4
  41.6 2.6 collective-permute-done.4
  44.1 4.4 %collective-permute-done.5 = bf16[1,4,128,256]{3,2,1,0:T(8,128)(2,1)S(1)} collective-permute-done((bf16[1,4,128,256]{3,2,1,0:T(8,128)(2,1)S(1)}, bf16[1,4,128,256]{3,2,1,0:T(8,128)(2,1)S(1)}, u32[]{:S(2)}, u32[]{:S(2)}) %collective-permute-start.5) | collective-permute-done | bytes 262176 | tf_op jit(solution)/shard_map/ppermute | solution.py:20
  49.3 5.3 %collective-permute-start.6 = (bf16[3,1,128,256]{3,2,1,0:T(8,128)(2,1)}, bf16[3,1,128,256]{3,2,1,0:T(8,128)(2,1)}, u32[]{:S(2)}, u32[]{:S(2)}) collective-permute-start(bf16[3,1,128,256]{3,2,1,0:T(8,128)(2,1)} %get-tuple-element.248), channel_id=1, source_target_pairs={{0,1},{1,2},{2,3},{3,4},{4,5},{5,6},{6,7},{8,9},{9,10},{10,11},{11... | collective-permute-start | bytes 589832 | tf_op jit(solution)/shard_map/ppermute | solution.py:18
  56.1 1.6 fusion.101
  70.9 2.2 fusion.98
  73.8 15.0 %all_gather.6 = bf16[1024,128]{1,0:T(8,128)(2,1)S(1)} all-gather(bf16[128,128]{1,0:T(8,128)(2,1)S(1)} %fusion.31), channel_id=1, replica_groups=mesh['aa'=4,'ba'=8] {'ba'}, dimensions={0}, use_global_device_ids=true | all-gather | bytes 294912 | tf_op jit(solution)/shard_map/all_gather | solution.py:149
  92.1 4.3 %fusion.25 = bf16[1024,768]{0,1:T(8,128)(2,1)S(1)} fusion(bf16[2048,256]{1,0:T(8,128)(2,1)S(1)} %copy-done.20, bf16[2048,256]{1,0:T(8,128)(2,1)S(1)} %copy-done.21, bf16[2048,256]{1,0:T(8,128)(2,1)S(1)} %copy-done.22, f32[1024,2048]{1,0:T(8,128)S(1)} %get-tuple-element.257, f32[2048]{0:T(1024)S(1)} %copy-done.23, f32[1024]{0:T(1024)S(1)} %add_rsqrt_fusion, ...), kind=kOutput, calls=%fused_computation.33 | convolution fusion | flops 3241934848 | bytes 13131776 | tf_op jit(solution)/shard_map/dot_general | solution.py:147
  96.8 13.9 %collective-permute-done.8 = bf16[1024,256]{0,1:T(8,128)(2,1)S(1)} collective-permute-done((bf16[1024,256]{0,1:T(8,128)(2,1)S(1)}, bf16[1024,256]{0,1:T(8,128)(2,1)S(1)}, u32[]{:S(2)}, u32[]{:S(2)}) %collective-permute-start.8) | collective-permute-done | bytes 524320 | tf_op jit(solution)/shard_map/ppermute | solution.py:81
  112.1 46.6 %collective-permute-done.9 = bf16[2048,256]{0,1:T(8,128)(2,1)S(1)} collective-permute-done((bf16[2048,256]{0,1:T(8,128)(2,1)S(1)}, bf16[2048,256]{0,1:T(8,128)(2,1)S(1)}, u32[]{:S(2)}, u32[]{:S(2)}) %collective-permute-start.9) | collective-permute-done | bytes 1048608 | tf_op jit(solution)/shard_map/ppermute | solution.py:81
  159.8 2.0 copy-done.3
  164.1 3.1 constant_dynamic-slice_fusion.2
  167.2 39.1 %all-gather.2.cloned.1.call-done = bf16[4096,256]{0,1:T(8,128)(2,1)} async-done(((bf16[1024,256]{0,1:T(8,128)(2,1)}), bf16[4096,256]{0,1:T(8,128)(2,1)}) %all-gather.2.cloned.1.call-update) | async-done | bytes 2097168 | tf_op jit(solution)/shard_map/all_gather | solution.py:91
  206.3 101.7 %while.18 = (s32[]{:T(128)}, f32[4,1024]{1,0:T(4,128)S(1)}, f32[4,1024]{1,0:T(4,128)S(1)}, f32[1024,4,64]{0,2,1:T(8,128)S(1)}, bf16[4096,256]{0,1:T(8,128)(2,1)}...) while((s32[]{:T(128)}, f32[4,1024]{1,0:T(4,128)S(1)}, ...), condition=%wide.region_5.6_spmd.clone, body=%wide.region_2.5_spmd.clone.sunk | while | flops 1108107264 | bytes 56361128 | solution.py:119
  207.6 8.1 %bitcast_reduce_fusion.2 = (f32[4,1024]{1,0:T(4,128)S(1)}, f32[4,1024,1024]{2,1,0:T(8,128)}) fusion(bf16[1024,4,64]{0,2,1:T(8,128)(2,1)S(1)} %bitcast.131, bf16[1024,4,64]{0,2,1:T(8,128)(2,1)S(1)} %get-tuple-element.342), kind=kOutput, calls=%fused_computation.1.clone.1 | convolution fusion | flops 545255424 | bytes 17842176 | tf_op jit(solution)/shard_map/while/body/eval_jaxpr/qhd,khd->hqk/dot_general | solution.py:104
  215.7 7.4 %fusion.169 = f32[1024,4,64]{0,2,1:T(8,128)S(1)} fusion(bf16[1024,4,64]{0,2,1:T(8,128)(2,1)S(1)} %bitcast.132, f32[4,1024,1024]{2,1,0:T(8,128)} %get-tuple-element.312, f32[4,1024]{1,0:T(4,128)S(1)} %get-tuple-element.338, f32[1024,4,64]{0,2,1:T(8,128)S(1)} %get-tuple-element.329, f32[1024,4]{0,1:T(4,128)S(1)} %get-tuple-element.314, pred[]{:T(512)S(6)} %compare.44), kind=kOutput, calls=%fused_computation.7.clone.1 | convolution fusion | flops 550240256 | bytes 19431424 | tf_op jit(solution)/shard_map/while/body/eval_jaxpr/hqk,khd->qhd/dot_general | solution.py:111
  223.1 8.5 %fusion.167 = f32[4,1024]{1,0:T(4,128)S(1)} fusion(f32[4,1024,1024]{2,1,0:T(8,128)} %get-tuple-element.312, f32[4,1024]{1,0:T(4,128)S(1)} %get-tuple-element.338), kind=kLoop, calls=%fused_computation.4.clone.1 | loop fusion | flops 12578816 | bytes 16809984 | tf_op jit(solution)/shard_map/while/body/eval_jaxpr/reduce_sum | solution.py:110
  233.0 8.1 %bitcast_reduce_fusion.2 = (f32[4,1024]{1,0:T(4,128)S(1)}, f32[4,1024,1024]{2,1,0:T(8,128)}) fusion(bf16[1024,4,64]{0,2,1:T(8,128)(2,1)S(1)} %bitcast.131, bf16[1024,4,64]{0,2,1:T(8,128)(2,1)S(1)} %get-tuple-element.342), kind=kOutput, calls=%fused_computation.1.clone.1 | convolution fusion | flops 545255424 | bytes 17842176 | tf_op jit(solution)/shard_map/while/body/eval_jaxpr/qhd,khd->hqk/dot_general | solution.py:104
  241.2 7.4 %fusion.169 = f32[1024,4,64]{0,2,1:T(8,128)S(1)} fusion(bf16[1024,4,64]{0,2,1:T(8,128)(2,1)S(1)} %bitcast.132, f32[4,1024,1024]{2,1,0:T(8,128)} %get-tuple-element.312, f32[4,1024]{1,0:T(4,128)S(1)} %get-tuple-element.338, f32[1024,4,64]{0,2,1:T(8,128)S(1)} %get-tuple-element.329, f32[1024,4]{0,1:T(4,128)S(1)} %get-tuple-element.314, pred[]{:T(512)S(6)} %compare.44), kind=kOutput, calls=%fused_computation.7.clone.1 | convolution fusion | flops 550240256 | bytes 19431424 | tf_op jit(solution)/shard_map/while/body/eval_jaxpr/hqk,khd->qhd/dot_general | solution.py:111
  248.6 8.5 %fusion.167 = f32[4,1024]{1,0:T(4,128)S(1)} fusion(f32[4,1024,1024]{2,1,0:T(8,128)} %get-tuple-element.312, f32[4,1024]{1,0:T(4,128)S(1)} %get-tuple-element.338), kind=kLoop, calls=%fused_computation.4.clone.1 | loop fusion | flops 12578816 | bytes 16809984 | tf_op jit(solution)/shard_map/while/body/eval_jaxpr/reduce_sum | solution.py:110
  258.4 8.1 %bitcast_reduce_fusion.2 = (f32[4,1024]{1,0:T(4,128)S(1)}, f32[4,1024,1024]{2,1,0:T(8,128)}) fusion(bf16[1024,4,64]{0,2,1:T(8,128)(2,1)S(1)} %bitcast.131, bf16[1024,4,64]{0,2,1:T(8,128)(2,1)S(1)} %get-tuple-element.342), kind=kOutput, calls=%fused_computation.1.clone.1 | convolution fusion | flops 545255424 | bytes 17842176 | tf_op jit(solution)/shard_map/while/body/eval_jaxpr/qhd,khd->hqk/dot_general | solution.py:104
  266.6 7.4 %fusion.169 = f32[1024,4,64]{0,2,1:T(8,128)S(1)} fusion(bf16[1024,4,64]{0,2,1:T(8,128)(2,1)S(1)} %bitcast.132, f32[4,1024,1024]{2,1,0:T(8,128)} %get-tuple-element.312, f32[4,1024]{1,0:T(4,128)S(1)} %get-tuple-element.338, f32[1024,4,64]{0,2,1:T(8,128)S(1)} %get-tuple-element.329, f32[1024,4]{0,1:T(4,128)S(1)} %get-tuple-element.314, pred[]{:T(512)S(6)} %compare.44), kind=kOutput, calls=%fused_computation.7.clone.1 | convolution fusion | flops 550240256 | bytes 19431424 | tf_op jit(solution)/shard_map/while/body/eval_jaxpr/hqk,khd->qhd/dot_general | solution.py:111
  274.0 8.5 %fusion.167 = f32[4,1024]{1,0:T(4,128)S(1)} fusion(f32[4,1024,1024]{2,1,0:T(8,128)} %get-tuple-element.312, f32[4,1024]{1,0:T(4,128)S(1)} %get-tuple-element.338), kind=kLoop, calls=%fused_computation.4.clone.1 | loop fusion | flops 12578816 | bytes 16809984 | tf_op jit(solution)/shard_map/while/body/eval_jaxpr/reduce_sum | solution.py:110
  283.8 8.1 %bitcast_reduce_fusion.2 = (f32[4,1024]{1,0:T(4,128)S(1)}, f32[4,1024,1024]{2,1,0:T(8,128)}) fusion(bf16[1024,4,64]{0,2,1:T(8,128)(2,1)S(1)} %bitcast.131, bf16[1024,4,64]{0,2,1:T(8,128)(2,1)S(1)} %get-tuple-element.342), kind=kOutput, calls=%fused_computation.1.clone.1 | convolution fusion | flops 545255424 | bytes 17842176 | tf_op jit(solution)/shard_map/while/body/eval_jaxpr/qhd,khd->hqk/dot_general | solution.py:104
  292.0 7.4 %fusion.169 = f32[1024,4,64]{0,2,1:T(8,128)S(1)} fusion(bf16[1024,4,64]{0,2,1:T(8,128)(2,1)S(1)} %bitcast.132, f32[4,1024,1024]{2,1,0:T(8,128)} %get-tuple-element.312, f32[4,1024]{1,0:T(4,128)S(1)} %get-tuple-element.338, f32[1024,4,64]{0,2,1:T(8,128)S(1)} %get-tuple-element.329, f32[1024,4]{0,1:T(4,128)S(1)} %get-tuple-element.314, pred[]{:T(512)S(6)} %compare.44), kind=kOutput, calls=%fused_computation.7.clone.1 | convolution fusion | flops 550240256 | bytes 19431424 | tf_op jit(solution)/shard_map/while/body/eval_jaxpr/hqk,khd->qhd/dot_general | solution.py:111
  299.4 8.5 %fusion.167 = f32[4,1024]{1,0:T(4,128)S(1)} fusion(f32[4,1024,1024]{2,1,0:T(8,128)} %get-tuple-element.312, f32[4,1024]{1,0:T(4,128)S(1)} %get-tuple-element.338), kind=kLoop, calls=%fused_computation.4.clone.1 | loop fusion | flops 12578816 | bytes 16809984 | tf_op jit(solution)/shard_map/while/body/eval_jaxpr/reduce_sum | solution.py:110
  309.9 32.6 %reduce-scatter.2.cloned.1.call-done = bf16[128,128]{1,0:T(8,128)(2,1)} async-done(((bf16[1024,128]{1,0:T(8,128)(2,1)}), bf16[128,128]{1,0:T(8,128)(2,1)}) %reduce-scatter.2.cloned.1.call-update) | async-done | bytes 32784 | tf_op jit(solution)/shard_map/reduce_scatter | solution.py:155
  (140 shorter events, 47.1 us)
Async XLA Ops:
  6.5 82.3 %copy-start = (bf16[128,2048]{1,0:T(8,128)(2,1)S(1)}, bf16[128,2048]{1,0:T(8,128)(2,1)}, u32[]{:S(2)}) copy-start(bf16[128,2048]{1,0:T(8,128)(2,1)} %param.23) | copy-start | bytes 1572868
  6.5 199.8 %all-gather.2.cloned.1.call-start = ((), (), s32[]{:S(2)}) async-start(), calls=%async_computation.1 | async-start | bytes 2621440 | tf_op jit(solution)/shard_map/all_gather | solution.py:91
  6.5 10.9 %collective-permute-start = (bf16[1,4,128,256]{3,2,1,0:T(8,128)(2,1)}, bf16[1,4,128,256]{3,2,1,0:T(8,128)(2,1)S(1)}, u32[]{:S(2)}, u32[]{:S(2)}) collective-permute-start(bf16[1,4,128,256]{3,2,1,0:T(8,128)(2,1)} %param.16), channel_id=1, source_target_pairs={{0,8},{8,16},{16,24},{1,9},{9,17},{17,25},{2,10},{10,18},{18,26},{... | collective-permute-start | bytes 786440 | tf_op jit(solution)/shard_map/ppermute | solution.py:18
  11.6 9.9 %collective-permute-start.1 = (bf16[1,4,128,256]{3,2,1,0:T(8,128)(2,1)}, bf16[1,4,128,256]{3,2,1,0:T(8,128)(2,1)S(1)}, u32[]{:S(2)}, u32[]{:S(2)}) collective-permute-start(bf16[1,4,128,256]{3,2,1,0:T(8,128)(2,1)} %param.16), channel_id=1, source_target_pairs={{8,0},{16,8},{24,16},{9,1},{17,9},{25,17},{10,2},{18,10},{26,18},{... | collective-permute-start | bytes 786440 | tf_op jit(solution)/shard_map/ppermute | solution.py:20
  21.6 4.8 %collective-permute-start.2 = (bf16[3,1,128,256]{3,2,1,0:T(8,128)(2,1)S(1)}, bf16[3,1,128,256]{3,2,1,0:T(8,128)(2,1)S(1)}, u32[]{:S(2)}, u32[]{:S(2)}) collective-permute-start(bf16[3,1,128,256]{3,2,1,0:T(8,128)(2,1)S(1)} %get-tuple-element.250), channel_id=1, source_target_pairs={{0,1},{1,2},{2,3},{3,4},{4,5},{5,6},{6,7},{8,9},{9,10},{10,11},{11... | collective-permute-start | bytes 589832 | tf_op jit(solution)/shard_map/ppermute | solution.py:18
  22.9 5.1 %collective-permute-start.3 = (bf16[3,1,128,256]{3,2,1,0:T(8,128)(2,1)S(1)}, bf16[3,1,128,256]{3,2,1,0:T(8,128)(2,1)S(1)}, u32[]{:S(2)}, u32[]{:S(2)}) collective-permute-start(bf16[3,1,128,256]{3,2,1,0:T(8,128)(2,1)S(1)} %get-tuple-element.249), channel_id=1, source_target_pairs={{1,0},{2,1},{3,2},{4,3},{5,4},{6,5},{7,6},{9,8},{10,9},{11,10},{12... | collective-permute-start | bytes 589832 | tf_op jit(solution)/shard_map/ppermute | solution.py:20
  33.5 22.6 %copy-start.2 = (bf16[3,3,3,256,256]{4,3,2,1,0:T(8,128)(2,1)S(1)}, bf16[3,3,3,256,256]{4,3,2,1,0:T(8,128)(2,1)}, u32[]{:S(2)}) copy-start(bf16[3,3,3,256,256]{4,3,2,1,0:T(8,128)(2,1)} %param.19) | copy-start | bytes 10616836
  36.8 7.3 %collective-permute-start.4 = (bf16[1,4,128,256]{3,2,1,0:T(8,128)(2,1)S(1)}, bf16[1,4,128,256]{3,2,1,0:T(8,128)(2,1)S(1)}, u32[]{:S(2)}, u32[]{:S(2)}) collective-permute-start(bf16[1,4,128,256]{3,2,1,0:T(8,128)(2,1)S(1)} %fusion.66), channel_id=1, source_target_pairs={{0,8},{8,16},{16,24},{1,9},{9,17},{17,25},{2,10},{10,18},{18,26},{... | collective-permute-start | bytes 786440 | tf_op jit(solution)/shard_map/ppermute | solution.py:18
  40.3 8.3 %collective-permute-start.5 = (bf16[1,4,128,256]{3,2,1,0:T(8,128)(2,1)S(1)}, bf16[1,4,128,256]{3,2,1,0:T(8,128)(2,1)S(1)}, u32[]{:S(2)}, u32[]{:S(2)}) collective-permute-start(bf16[1,4,128,256]{3,2,1,0:T(8,128)(2,1)S(1)} %fusion.66), channel_id=1, source_target_pairs={{8,0},{16,8},{24,16},{9,1},{17,9},{25,17},{10,2},{18,10},{26,18},{... | collective-permute-start | bytes 786440 | tf_op jit(solution)/shard_map/ppermute | solution.py:20
  49.3 9.0 %collective-permute-start.6 = (bf16[3,1,128,256]{3,2,1,0:T(8,128)(2,1)}, bf16[3,1,128,256]{3,2,1,0:T(8,128)(2,1)}, u32[]{:S(2)}, u32[]{:S(2)}) collective-permute-start(bf16[3,1,128,256]{3,2,1,0:T(8,128)(2,1)} %get-tuple-element.248), channel_id=1, source_target_pairs={{0,1},{1,2},{2,3},{3,4},{4,5},{5,6},{6,7},{8,9},{9,10},{10,11},{11... | collective-permute-start | bytes 589832 | tf_op jit(solution)/shard_map/ppermute | solution.py:18
  54.6 5.0 %collective-permute-start.7 = (bf16[3,1,128,256]{3,2,1,0:T(8,128)(2,1)}, bf16[3,1,128,256]{3,2,1,0:T(8,128)(2,1)S(1)}, u32[]{:S(2)}, u32[]{:S(2)}) collective-permute-start(bf16[3,1,128,256]{3,2,1,0:T(8,128)(2,1)} %get-tuple-element.247), channel_id=1, source_target_pairs={{1,0},{2,1},{3,2},{4,3},{5,4},{6,5},{7,6},{9,8},{10,9},{11,10},{12... | collective-permute-start | bytes 589832 | tf_op jit(solution)/shard_map/ppermute | solution.py:20
  59.7 2.4 copy-start.12
  62.1 1.1 copy-start.10
  63.3 1.0 copy-start.9
  64.6 1.0 copy-start.8
  64.9 1.1 copy-start.7
  66.0 1.1 copy-start.25
  66.4 1.0 copy-start.6
  67.5 1.0 copy-start.5
  68.8 1.0 copy-start.18
  70.9 2.7 copy-start.15
  70.9 2.7 copy-start.19
  70.9 17.9 %copy-start.16 = (f32[2048]{0:T(1024)S(1)}, f32[2048]{0:T(1024)}, u32[]{:S(2)}) copy-start(f32[2048]{0:T(1024)} %param.24) | copy-start | bytes 24580
  90.2 1.3 copy-start.20
  90.2 1.5 copy-start.21
  90.2 1.8 copy-start.22
  90.2 1.8 copy-start.23
  96.4 14.2 %collective-permute-start.8 = (bf16[1024,256]{0,1:T(8,128)(2,1)S(1)}, bf16[1024,256]{0,1:T(8,128)(2,1)S(1)}, u32[]{:S(2)}, u32[]{:S(2)}) collective-permute-start(bf16[1024,256]{0,1:T(8,128)(2,1)S(1)} %get-tuple-element.197), channel_id=1, source_target_pairs={{0,24},{8,0},{16,8},{24,16},{1,25},{9,1},{17,9},{25,17},{2,26},{10... | collective-permute-start | bytes 1572872 | tf_op jit(solution)/shard_map/ppermute | solution.py:81
  110.8 48.0 %collective-permute-start.9 = (bf16[2048,256]{0,1:T(8,128)(2,1)S(1)}, bf16[2048,256]{0,1:T(8,128)(2,1)S(1)}, u32[]{:S(2)}, u32[]{:S(2)}) collective-permute-start(bf16[2048,256]{0,1:T(8,128)(2,1)S(1)} %pad_maximum_fusion), channel_id=1, source_target_pairs={{0,16},{8,24},{16,0},{24,8},{1,17},{9,25},{17,1},{25,9},{2,18},{10... | collective-permute-start | bytes 3145736 | tf_op jit(solution)/shard_map/ppermute | solution.py:81
  159.8 2.0 copy-start.3
  161.7 180.8 %reduce-scatter.2.cloned.1.call-start = ((), (), s32[]{:S(2)}) async-start(), calls=%async_computation.2 | async-start | bytes 294912 | tf_op jit(solution)/shard_map/reduce_scatter | solution.py:155
  308.0 36.0 %copy-start.1 = (bf16[128,2048]{1,0:T(8,128)(2,1)S(1)}, bf16[128,2048]{1,0:T(8,128)(2,1)}, u32[]{:S(2)}) copy-start(bf16[128,2048]{1,0:T(8,128)(2,1)} %param.23) | copy-start | bytes 1572868
  (6 other events, 5.5 us)
Sparse Core Ops, SparseCore 0:
  161.9 44.4 all-gather.1
  310.0 32.4 reduce-scatter.1
